TPU v7x, 32 devices: a whole 2x2x4 slice. The times are simulated.
32 devices in a mesh: mem: 4 (over x, core), band: 8 (over z, y).
Axes of the slice: x: 2, y: 2, z: 4, core: 2. Of those that a mesh axis runs over, the one named last changes fastest.
Arguments:
- sample_collection: float32 [24, 3, 64, 4096], P('mem', None, 'band'), may hold values from -6 to 6
- seabed_profile: float32 [64, 4096], P('band'), may hold values from 0.5 to 2
- gauge_grid_position: int32 [32, 128], P('band'), may hold values from 0 to 262143, as said below
- observed_values: float32 [32, 128], P('band'), may hold values from -6 to 6
- error_scale: float32 [32, 128], P('band'), may hold values from 0.3 to 3
- perturbation: float32 [24, 32, 128], P('mem', 'band'), may hold values from -6 to 6
- inflation: float32 [1], replicated, may hold values from 1 to 16
Outputs:
- analysis: float32 [24, 3, 64, 4096], P('mem', None, 'band')
Inputs may be any that keep to these rules, and one draw needn't show every extreme that they name: Every entry in row r of gauge_grid_position lies in grid rows b * 8 to (b + 1) * 8 - 1 with b = r // 4; cells may repeat.
All inputs are finite; a program needn't handle non-finite values.
Results may differ from a plain program's by a relative error of at most 0.000071.
Values sent between devices are 32-bit elements; how exact they have to be, the bound alone decides.
No kernel may reach another device: no remote copies, remote signals or barrier semaphores. Data moves between devices by JAX's collectives and lax.ppermute only.
A program may use at most 128 MiB of HBM per device.

v0:
```python
import math
import jax
import jax.numpy as jnp
from jax import lax
from jax.sharding import PartitionSpec as P

STEPS = 2
courant = 0.5
coriolis_base = 0.15
coriolis_slope = 0.3


def with_halo(cells, sides, width):
    for axis, dim in sides:
        count = lax.axis_size(axis)
        ends = count - 1
        head = lax.slice_in_dim(cells, 0, width, axis=dim)
        tail = lax.slice_in_dim(cells, cells.shape[dim] - width, cells.shape[dim], axis=dim)
        cells = jnp.concatenate(
            [
                lax.ppermute(tail, axis, [(i, (i + 1) % count) for i in range(ends)]),
                cells,
                lax.ppermute(head, axis, [((i + 1) % count, i) for i in range(ends)]),
            ],
            axis=dim,
        )
    return cells


def east_diff(quantity):
    return (jnp.roll(quantity, -1, axis=-1) - jnp.roll(quantity, 1, axis=-1)) * 0.5


def body(
    sample_collection,
    seabed_profile,
    gauge_grid_position,
    observed_values,
    error_scale,
    perturbation,
    inflation,
):
    local_members, _, band_rows, columns = sample_collection.shape
    total_rows = band_rows * lax.axis_size("band")
    sample_trajectories = local_members * lax.axis_size("mem")
    first_row = lax.axis_index("band") * band_rows
    global_rows = (first_row + jnp.arange(band_rows)).astype(jnp.float32)
    earth_spin_turning = (coriolis_base + coriolis_slope * (global_rows + 0.5) / total_rows)[
        :, None
    ]
    surface_height, eastward_velocity_field, northward_velocity_field = (
        sample_collection[:, 0],
        sample_collection[:, 1],
        sample_collection[:, 2],
    )
    for _ in range(STEPS):
        rim_flux = with_halo(seabed_profile * northward_velocity_field, (("band", 1),), 1)
        surface_height = surface_height - courant * (
            east_diff(seabed_profile * eastward_velocity_field)
            + (rim_flux[:, 2:] - rim_flux[:, :-2]) * 0.5
        )
        eastward_velocity_field = (
            eastward_velocity_field
            - courant * east_diff(surface_height)
            + earth_spin_turning * northward_velocity_field
        )
        rim_height = with_halo(surface_height, (("band", 1),), 1)
        northward_velocity_field = (
            northward_velocity_field
            - courant * ((rim_height[:, 2:] - rim_height[:, :-2]) * 0.5)
            - earth_spin_turning * eastward_velocity_field
        )
    prior_model_outputs = jnp.stack(
        [surface_height, eastward_velocity_field, northward_velocity_field], axis=1
    )
    local_cells = gauge_grid_position.reshape(-1) - first_row * columns
    modelled_water_levels = jnp.take(surface_height.reshape(local_members, -1), local_cells, axis=1)
    obs_scale = error_scale.reshape(-1)
    factor = inflation[0]
    innovation = (
        observed_values.reshape(-1)
        + jnp.sqrt(factor) * obs_scale * perturbation.reshape(local_members, -1)
        - modelled_water_levels
    ) / obs_scale
    norm_factor = math.sqrt(sample_trajectories - 1)
    centre = lax.psum(jnp.sum(modelled_water_levels, axis=0), "mem") / sample_trajectories
    spread_local = (modelled_water_levels - centre) / (obs_scale * norm_factor)
    spread, innovation_all = (
        lax.all_gather(spread_local, "mem", axis=0, tiled=True),
        lax.all_gather(innovation, "mem", axis=0, tiled=True),
    )
    gram_local = jnp.dot(
        spread, spread.T, precision=lax.Precision.HIGHEST, preferred_element_type=jnp.float32
    )
    cross_local = jnp.dot(
        spread,
        innovation_all.T,
        precision=lax.Precision.HIGHEST,
        preferred_element_type=jnp.float32,
    )
    gram_matrix, cross_term = lax.psum((gram_local, cross_local), "band")
    system = gram_matrix + factor * jnp.eye(sample_trajectories, dtype=jnp.float32)
    cholesky_lower = jnp.linalg.cholesky(system)
    middle = lax.linalg.triangular_solve(cholesky_lower, cross_term, left_side=True, lower=True)
    weights = lax.linalg.triangular_solve(
        cholesky_lower, middle, left_side=True, lower=True, transpose_a=True
    )
    assimilate_update_step = (
        jnp.eye(sample_trajectories, dtype=jnp.float32)
        + (weights - jnp.mean(weights, axis=0, keepdims=True)) / norm_factor
    )
    own_rows = lax.dynamic_slice_in_dim(
        assimilate_update_step, lax.axis_index("mem") * local_members, local_members, 0
    )
    return lax.psum_scatter(
        jnp.tensordot(
            own_rows, prior_model_outputs, axes=([0], [0]), precision=lax.Precision.HIGHEST
        ),
        "mem",
        scatter_dimension=0,
        tiled=True,
    )


def solution(mesh):
    in_specs = (
        P("mem", None, "band", None),
        P("band", None),
        P("band", None),
        P("band", None),
        P("band", None),
        P("mem", "band", None),
        P(),
    )
    out_specs = P("mem", None, "band", None)
    return jax.shard_map(body, mesh=mesh, in_specs=in_specs, out_specs=out_specs, check_vma=False)
```

profile of v0, /device:TPU:0, one launch (start us, length us, event | category | flops | bytes accessed | tf_op | source)
XLA Modules:
  0.0 242.2 jit_solution(15384957077126619160)
XLA Ops:
  6.5 2.7 %fusion.57 = (f32[6,1,8,4096]{3,2,1,0:T(8,128)}, f32[6,1,8,4096]{3,2,1,0:T(8,128)S(1)}, f32[6,1,8,4096]{3,2,1,0:T(8,128)S(1)}) fusion(f32[6,3,8,4096]{3,2,1,0:T(8,128)} %param.7), kind=kLoop, calls=%fused_computation.92 | loop fusion | bytes 4718592 | tf_op jit(solution)/shard_map/slice | solution.py:52
  10.3 1.3 collective-permute-start
  11.6 5.5 %collective-permute-start.1 = (f32[6,1,4096]{2,0,1:T(8,128)S(1)}, f32[6,1,4096]{2,0,1:T(8,128)S(1)}, u32[]{:S(2)}, u32[]{:S(2)}) collective-permute-start(f32[6,1,4096]{2,0,1:T(8,128)S(1)} %get-tuple-element.41), channel_id=1, source_target_pairs={{0,1},{1,2},{2,3},{3,4},{4,5},{5,6},{6,7},{8,9},{9,10},{10,11},{11... | collective-permute-start | bytes 294920 | tf_op jit(solution)/shard_map/ppermute | solution.py:21
  17.1 1.7 fusion.68
  20.6 1.1 collective-permute-done.1
  21.7 2.6 %fusion.22 = f32[6,8,4096]{2,0,1:T(8,128)S(1)} fusion(f32[6,8,4096]{2,0,1:T(8,128)S(1)} %get-tuple-element.45, f32[6,1,4096]{2,0,1:T(8,128)S(1)} %collective-permute-done.1, f32[6,1,4096]{2,0,1:T(8,128)S(1)} %collective-permute-done, f32[6,8,1]{2,0,1:T(8,128)S(1)} %get-tuple-element.37, f32[6,8,4095]{2,0,1:T(8,128)} %get-tuple-element.39, ...), kind=kLoop, calls=%fused_computation.30 | loop fusion | flops 1769472 | bytes 4128768 | tf_op jit(solution)/shard_map/sub | solution.py:58
  24.7 1.3 collective-permute-start.2
  26.0 5.0 %collective-permute-start.3 = (f32[6,1,4096]{2,0,1:T(8,128)S(1)}, f32[6,1,4096]{2,0,1:T(8,128)S(1)}, u32[]{:S(2)}, u32[]{:S(2)}) collective-permute-start(f32[6,1,4096]{2,0,1:T(8,128)S(1)} %get-tuple-element.31), channel_id=1, source_target_pairs={{0,1},{1,2},{2,3},{3,4},{4,5},{5,6},{6,7},{8,9},{9,10},{10,11},{11... | collective-permute-start | bytes 294920 | tf_op jit(solution)/shard_map/ppermute | solution.py:21
  31.1 1.3 broadcast_multiply_fusion.1
  32.8 3.0 %collective-permute-done.3 = f32[6,1,4096]{2,0,1:T(8,128)S(1)} collective-permute-done((f32[6,1,4096]{2,0,1:T(8,128)S(1)}, f32[6,1,4096]{2,0,1:T(8,128)S(1)}, u32[]{:S(2)}, u32[]{:S(2)}) %collective-permute-start.3) | collective-permute-done | bytes 98336 | tf_op jit(solution)/shard_map/ppermute | solution.py:21
  36.5 1.3 collective-permute-start.4
  37.8 5.0 %collective-permute-start.5 = (f32[6,1,4096]{2,0,1:T(8,128)S(1)}, f32[6,1,4096]{2,0,1:T(8,128)S(1)}, u32[]{:S(2)}, u32[]{:S(2)}) collective-permute-start(f32[6,1,4096]{2,0,1:T(8,128)S(1)} %get-tuple-element.29), channel_id=1, source_target_pairs={{0,1},{1,2},{2,3},{3,4},{4,5},{5,6},{6,7},{8,9},{9,10},{10,11},{11... | collective-permute-start | bytes 294920 | tf_op jit(solution)/shard_map/ppermute | solution.py:21
  42.9 1.7 collective-permute-done.4
  44.6 3.0 %collective-permute-done.5 = f32[6,1,4096]{2,0,1:T(8,128)S(1)} collective-permute-done((f32[6,1,4096]{2,0,1:T(8,128)S(1)}, f32[6,1,4096]{2,0,1:T(8,128)S(1)}, u32[]{:S(2)}, u32[]{:S(2)}) %collective-permute-start.5) | collective-permute-done | bytes 98336 | tf_op jit(solution)/shard_map/ppermute | solution.py:21
  48.0 1.6 fusion.58
  50.5 9.0 %copy.26 = f32[6,32768]{0,1:T(8,128)} copy(f32[6,32768]{1,0:T(8,128)S(1)} %bitcast.84) | data formatting | bytes 1572864 | tf_op jit(solution)/shard_map/reshape | solution.py:77
  59.5 6.8 %gather_fusion = f32[512,6]{1,0:T(8,128)S(1)} fusion(f32[6,32768]{0,1:T(8,128)} %copy.26, s32[1024]{0:T(1024)S(1)} %pad_clamp_fusion), kind=kCustom, calls=%fused_computation | custom fusion | bytes 26624 | tf_op jit(solution)/shard_map/jit(_take)/gather | solution.py:77
  66.5 6.9 %psum.21 = f32[512]{0:T(512)S(1)} all-reduce(f32[512]{0:T(512)S(1)} %select_reduce_fusion), channel_id=1, replica_groups=mesh['mem'=4,'band'=8] {'mem'}, use_global_device_ids=true, to_apply=%region_1.2 | all-reduce | flops 512 | bytes 4096 | tf_op jit(solution)/shard_map/psum | solution.py:86
  73.4 2.2 fusion.34
  75.6 1.1 copy.27
  76.7 5.2 %all-gather = f32[4,6,512]{2,1,0:T(8,128)S(1)} all-gather(f32[1,6,512]{2,1,0:T(8,128)S(1)} %copy.27), channel_id=1, replica_groups=mesh['mem'=4,'band'=8] {'mem'}, dimensions={0}, use_global_device_ids=true | all-gather | bytes 61440 | tf_op jit(solution)/shard_map/all_gather | solution.py:89
  83.0 5.2 %all-gather.1 = f32[4,6,512]{2,1,0:T(8,128)S(1)} all-gather(f32[1,6,512]{2,1,0:T(8,128)S(1)} %copy.30), channel_id=1, replica_groups=mesh['mem'=4,'band'=8] {'mem'}, dimensions={0}, use_global_device_ids=true | all-gather | bytes 61440 | tf_op jit(solution)/shard_map/all_gather | solution.py:90
  88.6 35.7 %all-reduce = (f32[24,24]{1,0:T(8,128)S(1)}, f32[24,24]{1,0:T(8,128)S(1)}) all-reduce(f32[24,24]{1,0:T(8,128)S(1)} %fusion.72, f32[24,24]{1,0:T(8,128)S(1)} %fusion.71), channel_id=1, replica_groups=mesh['mem'=4,'band'=8] {'band'}, use_global_device_ids=true, to_apply=%region_5.6 | all-reduce | flops 1152 | bytes 9216 | tf_op jit(solution)/shard_map/psum | solution.py:101
  124.3 2.2 cholesky.13
  127.7 1.8 custom-call.8
  130.0 1.3 collective-permute-start.6
  131.3 4.7 %collective-permute-start.7 = (f32[6,1,4096]{2,0,1:T(8,128)}, f32[6,1,4096]{2,0,1:T(8,128)S(1)}, u32[]{:S(2)}, u32[]{:S(2)}) collective-permute-start(f32[6,1,4096]{2,0,1:T(8,128)} %get-tuple-element.23), channel_id=1, source_target_pairs={{0,1},{1,2},{2,3},{3,4},{4,5},{5,6},{6,7},{8,9},{9,10},{10,11},{11... | collective-permute-start | bytes 294920 | tf_op jit(solution)/shard_map/ppermute | solution.py:21
  137.0 1.6 collective-permute-done.7
  138.6 2.1 fusion.10
  140.8 8.1 %fusion = f32[24,3,8,4096]{3,0,2,1:T(8,128)S(1)} fusion(f32[6,1,8,4096]{3,0,2,1:T(8,128)S(1)} %get-tuple-element.9, f32[6,1,8,4096]{3,0,2,1:T(8,128)S(1)} %bitcast.86, f32[6,1,8,4096]{3,0,2,1:T(8,128)S(1)} %bitcast.85, f32[24,24]{1,0:T(8,128)S(1)} %get-tuple-element.49, s32[]{:T(128)S(6)} %select_n.31, pred[24,24]{1,0:T(8,128)(4,1)S(1)} %iota_compare_fusion.1, ...), kind=kOutput, calls=%fused_computation.1 | convolution fusion | flops 171049536 | bytes 12588548 | tf_op jit(solution)/shard_map/dot_general | solution.py:116
  148.8 9.1 %copy.31 = f32[24,3,8,4096]{3,2,1,0:T(8,128)} copy(f32[24,3,8,4096]{3,0,2,1:T(8,128)S(1)} %fusion) | data formatting | bytes 18874368 | tf_op jit(solution)/shard_map/dot_general | solution.py:116
  158.0 77.3 %reduce-scatter.2.cloned.1.call-done = f32[6,3,8,4096]{3,2,1,0:T(8,128)} async-done(((f32[24,3,8,4096]{3,2,1,0:T(8,128)}), f32[6,3,8,4096]{3,2,1,0:T(8,128)}) %reduce-scatter.2.cloned.1.call-update) | async-done | bytes 2359312 | tf_op jit(solution)/shard_map/reduce_scatter | solution.py:115
  (51 shorter events, 9.4 us)
Async XLA Ops:
  6.5 2.8 %copy-start = (f32[8,4096]{1,0:T(8,128)S(1)}, f32[8,4096]{1,0:T(8,128)}, u32[]{:S(2)}) copy-start(f32[8,4096]{1,0:T(8,128)} %param.8) | copy-start | bytes 393220
  6.5 228.8 %reduce-scatter.2.cloned.1.call-start = ((), (), s32[]{:S(2)}) async-start(), calls=%async_computation.1 | async-start | bytes 11796480 | tf_op jit(solution)/shard_map/reduce_scatter | solution.py:115
  10.2 8.7 %copy-start.4 = (s32[4,128]{1,0:T(4,128)S(1)}, s32[4,128]{1,0:T(4,128)}, u32[]{:S(2)}) copy-start(s32[4,128]{1,0:T(4,128)} %param.9) | copy-start | bytes 6148
  10.3 9.4 %copy-start.1 = (f32[6,4,128]{2,1,0:T(4,128)S(1)}, f32[6,4,128]{2,1,0:T(4,128)}, u32[]{:S(2)}) copy-start(f32[6,4,128]{2,1,0:T(4,128)} %param.12) | copy-start | bytes 36868
  10.3 10.3 %copy-start.2 = (f32[4,128]{1,0:T(4,128)S(1)}, f32[4,128]{1,0:T(4,128)}, u32[]{:S(2)}) copy-start(f32[4,128]{1,0:T(4,128)} %param.11) | copy-start | bytes 6148
  10.3 10.2 %collective-permute-start = (f32[6,1,4096]{2,0,1:T(8,128)S(1)}, f32[6,1,4096]{2,0,1:T(8,128)S(1)}, u32[]{:S(2)}, u32[]{:S(2)}) collective-permute-start(f32[6,1,4096]{2,0,1:T(8,128)S(1)} %get-tuple-element.40), channel_id=1, source_target_pairs={{1,0},{2,1},{3,2},{4,3},{5,4},{6,5},{7,6},{9,8},{10,9},{11,10},{12... | collective-permute-start | bytes 294920 | tf_op jit(solution)/shard_map/ppermute | solution.py:23
  11.6 10.1 %collective-permute-start.1 = (f32[6,1,4096]{2,0,1:T(8,128)S(1)}, f32[6,1,4096]{2,0,1:T(8,128)S(1)}, u32[]{:S(2)}, u32[]{:S(2)}) collective-permute-start(f32[6,1,4096]{2,0,1:T(8,128)S(1)} %get-tuple-element.41), channel_id=1, source_target_pairs={{0,1},{1,2},{2,3},{3,4},{4,5},{5,6},{6,7},{8,9},{9,10},{10,11},{11... | collective-permute-start | bytes 294920 | tf_op jit(solution)/shard_map/ppermute | solution.py:21
  24.7 8.1 %collective-permute-start.2 = (f32[6,1,4096]{2,0,1:T(8,128)S(1)}, f32[6,1,4096]{2,0,1:T(8,128)S(1)}, u32[]{:S(2)}, u32[]{:S(2)}) collective-permute-start(f32[6,1,4096]{2,0,1:T(8,128)S(1)} %get-tuple-element.30), channel_id=1, source_target_pairs={{1,0},{2,1},{3,2},{4,3},{5,4},{6,5},{7,6},{9,8},{10,9},{11,10},{12... | collective-permute-start | bytes 294920 | tf_op jit(solution)/shard_map/ppermute | solution.py:23
  26.0 9.7 %collective-permute-start.3 = (f32[6,1,4096]{2,0,1:T(8,128)S(1)}, f32[6,1,4096]{2,0,1:T(8,128)S(1)}, u32[]{:S(2)}, u32[]{:S(2)}) collective-permute-start(f32[6,1,4096]{2,0,1:T(8,128)S(1)} %get-tuple-element.31), channel_id=1, source_target_pairs={{0,1},{1,2},{2,3},{3,4},{4,5},{5,6},{6,7},{8,9},{9,10},{10,11},{11... | collective-permute-start | bytes 294920 | tf_op jit(solution)/shard_map/ppermute | solution.py:21
  36.5 8.1 %collective-permute-start.4 = (f32[6,1,4096]{2,0,1:T(8,128)S(1)}, f32[6,1,4096]{2,0,1:T(8,128)S(1)}, u32[]{:S(2)}, u32[]{:S(2)}) collective-permute-start(f32[6,1,4096]{2,0,1:T(8,128)S(1)} %get-tuple-element.28), channel_id=1, source_target_pairs={{1,0},{2,1},{3,2},{4,3},{5,4},{6,5},{7,6},{9,8},{10,9},{11,10},{12... | collective-permute-start | bytes 294920 | tf_op jit(solution)/shard_map/ppermute | solution.py:23
  37.8 9.7 %collective-permute-start.5 = (f32[6,1,4096]{2,0,1:T(8,128)S(1)}, f32[6,1,4096]{2,0,1:T(8,128)S(1)}, u32[]{:S(2)}, u32[]{:S(2)}) collective-permute-start(f32[6,1,4096]{2,0,1:T(8,128)S(1)} %get-tuple-element.29), channel_id=1, source_target_pairs={{0,1},{1,2},{2,3},{3,4},{4,5},{5,6},{6,7},{8,9},{9,10},{10,11},{11... | collective-permute-start | bytes 294920 | tf_op jit(solution)/shard_map/ppermute | solution.py:21
  50.5 22.9 %copy-start.3 = (f32[4,128]{1,0:T(4,128)S(1)}, f32[4,128]{1,0:T(4,128)}, u32[]{:S(2)}) copy-start(f32[4,128]{1,0:T(4,128)} %param.10) | copy-start | bytes 6148
  130.0 7.1 %collective-permute-start.6 = (f32[6,1,4096]{2,0,1:T(8,128)}, f32[6,1,4096]{2,0,1:T(8,128)S(1)}, u32[]{:S(2)}, u32[]{:S(2)}) collective-permute-start(f32[6,1,4096]{2,0,1:T(8,128)} %get-tuple-element.22), channel_id=1, source_target_pairs={{1,0},{2,1},{3,2},{4,3},{5,4},{6,5},{7,6},{9,8},{10,9},{11,10},{12... | collective-permute-start | bytes 294920 | tf_op jit(solution)/shard_map/ppermute | solution.py:23
  131.3 7.4 %collective-permute-start.7 = (f32[6,1,4096]{2,0,1:T(8,128)}, f32[6,1,4096]{2,0,1:T(8,128)S(1)}, u32[]{:S(2)}, u32[]{:S(2)}) collective-permute-start(f32[6,1,4096]{2,0,1:T(8,128)} %get-tuple-element.23), channel_id=1, source_target_pairs={{0,1},{1,2},{2,3},{3,4},{4,5},{5,6},{6,7},{8,9},{9,10},{10,11},{11... | collective-permute-start | bytes 294920 | tf_op jit(solution)/shard_map/ppermute | solution.py:21
Sparse Core Ops, SparseCore 0:
  158.1 77.1 reduce-scatter.1
where the time goes:
time: 243 us; the launch traced here: 242 us
  waiting for transfers between devices  88.8 us (37%)
  blocking collectives  53 us (22%)
  local copies, waits for them, and re-layouts  35.8 us (15%)
  starting transfers between devices  25.5 us (10%)
  other arithmetic  15.9 us (7%)
  between operations  14.3 us (6%)
  matrix products  8.79 us (4%)
    reduce_scatter x1, waiting for transfers between devices, body(): lax.psum_scatter(jnp.tensordot(own_rows, prior_model_outputs, axes=([0],...  77.3 us
    psum x1, blocking collectives, body(): gram_matrix, cross_term = lax.psum((gram_local, cross_local), 'band')  35.7 us
    ppermute x4, starting transfers between devices, with_halo(): lax.ppermute(tail, axis, [(i, (i + 1) % count) for i in range(ends)])  20.3 us
    dot_general x1, local copies, waits for them, and re-layouts, body(): jnp.tensordot(own_rows, prior_model_outputs, axes=([0], [0]), precision=l...  9.11 us
    reshape x1, local copies, waits for them, and re-layouts, body(): surface_height.reshape(local_members, -1)  8.99 us
    ppermute x4, waiting for transfers between devices, with_halo(): lax.ppermute(tail, axis, [(i, (i + 1) % count) for i in range(ends)])  8.62 us
    dot_general x1, matrix products, body(): jnp.tensordot(own_rows, prior_model_outputs, axes=([0], [0]), precision=l...  8.06 us
    psum x1, blocking collectives, body(): lax.psum(jnp.sum(modelled_water_levels, axis=0), 'mem')  6.87 us
  transfers between devices with their start and end apart: 9, of which 8 were waited for; matrix products, arithmetic and copies ran while one was open for 2% of the time, Pallas kernels for 0%

commit v1 on v0

--- a/solution.py
+++ b/solution.py
@@ -1,3 +1,4 @@
+import functools
 import math
 import jax
 import jax.numpy as jnp
@@ -8,6 +9,21 @@
 courant = 0.5
 coriolis_base = 0.15
 coriolis_slope = 0.3
+
+
+def kinds_extend(sample, dev_axis):
+    return jnp.concatenate(
+        lax.all_to_all(
+            jnp.stack([sample for _ in range(lax.axis_size(dev_axis))], 0),
+            dev_axis,
+            split_axis=0,
+            concat_axis=0,
+        ),
+        0,
+    )
+
+
+derive_tiles = functools.partial(kinds_extend, dev_axis="mem")
 
 
 def with_halo(cells, sides, width):
@@ -86,7 +102,7 @@
     centre = lax.psum(jnp.sum(modelled_water_levels, axis=0), "mem") / sample_trajectories
     spread_local = (modelled_water_levels - centre) / (obs_scale * norm_factor)
     spread, innovation_all = (
-        lax.all_gather(spread_local, "mem", axis=0, tiled=True),
+        derive_tiles(spread_local),
         lax.all_gather(innovation, "mem", axis=0, tiled=True),
     )
     gram_local = jnp.dot(

time: 243 us -> 234 us (0.963)
  blocking collectives: 53 us -> 49 us
    ppermute x4, waiting for transfers between devices: 2.8 us -> 9.94 us  [with_halo(): lax.ppermute(head, axis, [((i + 1) % count, i) for i in range(ends)])]
    ppermute x4, waiting for transfers between devices: 8.62 us -> 2.53 us  [with_halo(): lax.ppermute(tail, axis, [(i, (i + 1) % count) for i in range(ends)])]
    all_gather x1 -> x0, blocking collectives: 5.23 us -> none  [body(): lax.all_gather(spread_local, 'mem', axis=0, tiled=True)]
    ppermute x4, starting transfers between devices: 20.3 us -> 17 us  [with_halo(): lax.ppermute(tail, axis, [(i, (i + 1) % count) for i in range(ends)])]
    all_to_all x0 -> x1, starting transfers between devices: none -> 3.28 us  [kinds_extend(): lax.all_to_all(jnp.stack([sample for _ in range(lax.axis_size(dev_axis))]...]
    unnamed x15 -> x11, local copies, waits for them, and re-layouts: 3.03 us -> 0.03 us
    gather x1 -> x2, local copies, waits for them, and re-layouts: 6.8 us -> 6.91 us  [body(): jnp.take(surface_height.reshape(local_members, -1), local_cells, axis=1)]
  transfers between devices with their start and end apart: 9 -> 10, of which waited for: 8 -> 5; matrix products, arithmetic and copies ran while one was open for 2% -> 4% of each run, Pallas kernels for 0% -> 0%
where the time goes in v1:
time: 234 us; the launch traced here: 233 us
  waiting for transfers between devices  88.3 us (38%)
  blocking collectives  49 us (21%)
  local copies, waits for them, and re-layouts  33.8 us (14%)
  starting transfers between devices  25.5 us (11%)
  between operations  14.4 us (6%)
  other arithmetic  13.8 us (6%)
  matrix products  8.8 us (4%)
    reduce_scatter x1, waiting for transfers between devices, body(): lax.psum_scatter(jnp.tensordot(own_rows, prior_model_outputs, axes=([0],...  75.8 us
    psum x1, blocking collectives, body(): gram_matrix, cross_term = lax.psum((gram_local, cross_local), 'band')  38.1 us
    ppermute x4, starting transfers between devices, with_halo(): lax.ppermute(tail, axis, [(i, (i + 1) % count) for i in range(ends)])  17 us
    ppermute x4, waiting for transfers between devices, with_halo(): lax.ppermute(head, axis, [((i + 1) % count, i) for i in range(ends)])  9.94 us
    dot_general x1, local copies, waits for them, and re-layouts, body(): jnp.tensordot(own_rows, prior_model_outputs, axes=([0], [0]), precision=l...  9.34 us
    reshape x1, local copies, waits for them, and re-layouts, body(): surface_height.reshape(local_members, -1)  8.96 us
    dot_general x1, matrix products, body(): jnp.tensordot(own_rows, prior_model_outputs, axes=([0], [0]), precision=l...  8.06 us
    gather x2, local copies, waits for them, and re-layouts, body(): jnp.take(surface_height.reshape(local_members, -1), local_cells, axis=1)  6.91 us
  transfers between devices with their start and end apart: 10, of which 5 were waited for; matrix products, arithmetic and copies ran while one was open for 4% of the time, Pallas kernels for 0%

profile of v1, /device:TPU:0, one launch (start us, length us, event | category | flops | bytes accessed | tf_op | source)
XLA Modules:
  0.0 233.5 jit_solution(13909586901406182831)
XLA Ops:
  6.5 2.7 %fusion.57 = (f32[6,1,8,4096]{3,2,1,0:T(8,128)}, f32[6,1,8,4096]{3,2,1,0:T(8,128)S(1)}, f32[6,1,8,4096]{3,2,1,0:T(8,128)S(1)}) fusion(f32[6,3,8,4096]{3,2,1,0:T(8,128)} %param.7), kind=kLoop, calls=%fused_computation.92 | loop fusion | bytes 4718592 | tf_op jit(solution)/shard_map/slice | solution.py:68
  9.3 0.9 fusion.31
  10.3 4.9 %collective-permute-start.1 = (f32[6,1,4096]{2,0,1:T(8,128)S(1)}, f32[6,1,4096]{2,0,1:T(8,128)S(1)}, u32[]{:S(2)}, u32[]{:S(2)}) collective-permute-start(f32[6,1,4096]{2,0,1:T(8,128)S(1)} %get-tuple-element.41), channel_id=1, source_target_pairs={{0,1},{1,2},{2,3},{3,4},{4,5},{5,6},{6,7},{8,9},{9,10},{10,11},{11... | collective-permute-start | bytes 294920 | tf_op jit(solution)/shard_map/ppermute | solution.py:37
  15.2 1.3 collective-permute-start
  16.6 1.7 fusion.68
  19.0 3.0 %collective-permute-done = f32[6,1,4096]{2,0,1:T(8,128)S(1)} collective-permute-done((f32[6,1,4096]{2,0,1:T(8,128)S(1)}, f32[6,1,4096]{2,0,1:T(8,128)S(1)}, u32[]{:S(2)}, u32[]{:S(2)}) %collective-permute-start) | collective-permute-done | bytes 98336 | tf_op jit(solution)/shard_map/ppermute | solution.py:39
  22.1 2.6 %fusion.22 = f32[6,8,4096]{2,0,1:T(8,128)S(1)} fusion(f32[6,8,4096]{2,0,1:T(8,128)S(1)} %get-tuple-element.43, f32[6,1,4096]{2,0,1:T(8,128)S(1)} %collective-permute-done.1, f32[6,1,4096]{2,0,1:T(8,128)S(1)} %collective-permute-done, f32[6,8,1]{2,0,1:T(8,128)S(1)} %get-tuple-element.37, f32[6,8,4095]{2,0,1:T(8,128)} %get-tuple-element.39, ...), kind=kLoop, calls=%fused_computation.30 | loop fusion | flops 1769472 | bytes 4128768 | tf_op jit(solution)/shard_map/sub | solution.py:74
  25.1 4.3 %collective-permute-start.3 = (f32[6,1,4096]{2,0,1:T(8,128)S(1)}, f32[6,1,4096]{2,0,1:T(8,128)S(1)}, u32[]{:S(2)}, u32[]{:S(2)}) collective-permute-start(f32[6,1,4096]{2,0,1:T(8,128)S(1)} %get-tuple-element.31), channel_id=1, source_target_pairs={{0,1},{1,2},{2,3},{3,4},{4,5},{5,6},{6,7},{8,9},{9,10},{10,11},{11... | collective-permute-start | bytes 294920 | tf_op jit(solution)/shard_map/ppermute | solution.py:37
  29.5 1.3 collective-permute-start.2
  30.8 1.3 broadcast_multiply_fusion.1
  32.4 3.9 %collective-permute-done.2 = f32[6,1,4096]{2,0,1:T(8,128)S(1)} collective-permute-done((f32[6,1,4096]{2,0,1:T(8,128)S(1)}, f32[6,1,4096]{2,0,1:T(8,128)S(1)}, u32[]{:S(2)}, u32[]{:S(2)}) %collective-permute-start.2) | collective-permute-done | bytes 98336 | tf_op jit(solution)/shard_map/ppermute | solution.py:39
  36.3 0.7 broadcast_multiply_fusion
  37.1 4.0 %collective-permute-start.5 = (f32[6,1,4096]{2,0,1:T(8,128)S(1)}, f32[6,1,4096]{2,0,1:T(8,128)S(1)}, u32[]{:S(2)}, u32[]{:S(2)}) collective-permute-start(f32[6,1,4096]{2,0,1:T(8,128)S(1)} %get-tuple-element.29), channel_id=1, source_target_pairs={{0,1},{1,2},{2,3},{3,4},{4,5},{5,6},{6,7},{8,9},{9,10},{10,11},{11... | collective-permute-start | bytes 294920 | tf_op jit(solution)/shard_map/ppermute | solution.py:37
  41.1 1.3 collective-permute-start.4
  42.4 2.5 %collective-permute-done.5 = f32[6,1,4096]{2,0,1:T(8,128)S(1)} collective-permute-done((f32[6,1,4096]{2,0,1:T(8,128)S(1)}, f32[6,1,4096]{2,0,1:T(8,128)S(1)}, u32[]{:S(2)}, u32[]{:S(2)}) %collective-permute-start.5) | collective-permute-done | bytes 98336 | tf_op jit(solution)/shard_map/ppermute | solution.py:37
  45.0 3.0 %collective-permute-done.4 = f32[6,1,4096]{2,0,1:T(8,128)S(1)} collective-permute-done((f32[6,1,4096]{2,0,1:T(8,128)S(1)}, f32[6,1,4096]{2,0,1:T(8,128)S(1)}, u32[]{:S(2)}, u32[]{:S(2)}) %collective-permute-start.4) | collective-permute-done | bytes 98336 | tf_op jit(solution)/shard_map/ppermute | solution.py:39
  48.4 0.7 fusion.60
  49.2 1.6 fusion.58
  50.8 9.0 %copy.36 = f32[6,32768]{0,1:T(8,128)} copy(f32[6,32768]{1,0:T(8,128)S(1)} %bitcast.84) | data formatting | bytes 1572864 | tf_op jit(solution)/shard_map/reshape | solution.py:93
  59.8 6.8 %gather_fusion = f32[512,6]{1,0:T(8,128)S(1)} fusion(f32[6,32768]{0,1:T(8,128)} %copy.36, s32[1024]{0:T(1024)S(1)} %pad_clamp_fusion), kind=kCustom, calls=%fused_computation | custom fusion | bytes 26624 | tf_op jit(solution)/shard_map/jit(_take)/gather | solution.py:93
  66.7 5.7 %psum.21 = f32[512]{0:T(512)S(1)} all-reduce(f32[512]{0:T(512)S(1)} %select_reduce_fusion), channel_id=1, replica_groups=mesh['mem'=4,'band'=8] {'mem'}, use_global_device_ids=true, to_apply=%region_1.2 | all-reduce | flops 512 | bytes 4096 | tf_op jit(solution)/shard_map/psum | solution.py:102
  73.0 3.3 %all-to-all-start = ((f32[4,6,512]{2,1,0:T(8,128)}), f32[4,6,512]{2,1,0:T(8,128)S(1)}, u32[]{:S(2)}, u32[]{:S(2)}) async-start(f32[4,6,512]{2,1,0:T(8,128)} %stack.19), calls=%async_computation | async-start | bytes 131072 | tf_op jit(solution)/shard_map/all_to_all | solution.py:16
  76.5 3.8 %collective-permute-start.7 = (f32[6,1,4096]{2,0,1:T(8,128)}, f32[6,1,4096]{2,0,1:T(8,128)S(1)}, u32[]{:S(2)}, u32[]{:S(2)}) collective-permute-start(f32[6,1,4096]{2,0,1:T(8,128)} %get-tuple-element.23), channel_id=1, source_target_pairs={{0,1},{1,2},{2,3},{3,4},{4,5},{5,6},{6,7},{8,9},{9,10},{10,11},{11... | collective-permute-start | bytes 294920 | tf_op jit(solution)/shard_map/ppermute | solution.py:37
  80.2 1.3 collective-permute-start.6
  81.5 5.2 %all-gather = f32[4,6,512]{2,1,0:T(8,128)S(1)} all-gather(f32[1,6,512]{2,1,0:T(8,128)S(1)} %get-tuple-element.44), channel_id=1, replica_groups=mesh['mem'=4,'band'=8] {'mem'}, dimensions={0}, use_global_device_ids=true | all-gather | bytes 61440 | tf_op jit(solution)/shard_map/all_gather | solution.py:106
  87.2 38.1 %all-reduce = (f32[24,24]{1,0:T(8,128)S(1)}, f32[24,24]{1,0:T(8,128)S(1)}) all-reduce(f32[24,24]{1,0:T(8,128)S(1)} %fusion.72, f32[24,24]{1,0:T(8,128)S(1)} %fusion.71), channel_id=1, replica_groups=mesh['mem'=4,'band'=8] {'band'}, use_global_device_ids=true, to_apply=%region_5.6 | all-reduce | flops 1152 | bytes 9216 | tf_op jit(solution)/shard_map/psum | solution.py:117
  125.3 2.2 cholesky.13
  128.9 1.8 custom-call.8
  131.2 2.2 fusion.10
  133.4 8.1 %fusion = f32[24,3,8,4096]{3,0,2,1:T(8,128)S(1)} fusion(f32[6,1,8,4096]{3,0,2,1:T(8,128)S(1)} %get-tuple-element.9, f32[6,1,8,4096]{3,0,2,1:T(8,128)S(1)} %bitcast.86, f32[6,1,8,4096]{3,0,2,1:T(8,128)S(1)} %bitcast.85, f32[24,24]{1,0:T(8,128)S(1)} %get-tuple-element.49, s32[]{:T(128)S(6)} %select_n.33, pred[24,24]{1,0:T(8,128)(4,1)S(1)} %iota_compare_fusion.1, ...), kind=kOutput, calls=%fused_computation.1 | convolution fusion | flops 171049536 | bytes 12588548 | tf_op jit(solution)/shard_map/dot_general | solution.py:132
  141.5 9.3 %copy.39 = f32[24,3,8,4096]{3,2,1,0:T(8,128)} copy(f32[24,3,8,4096]{3,0,2,1:T(8,128)S(1)} %fusion) | data formatting | bytes 18874368 | tf_op jit(solution)/shard_map/dot_general | solution.py:132
  150.8 75.8 %reduce-scatter.2.cloned.1.call-done = f32[6,3,8,4096]{3,2,1,0:T(8,128)} async-done(((f32[24,3,8,4096]{3,2,1,0:T(8,128)}), f32[6,3,8,4096]{3,2,1,0:T(8,128)}) %reduce-scatter.2.cloned.1.call-update) | async-done | bytes 2359312 | tf_op jit(solution)/shard_map/reduce_scatter | solution.py:131
  (51 shorter events, 4.7 us)
Async XLA Ops:
  6.5 2.7 %copy-start = (f32[8,4096]{1,0:T(8,128)S(1)}, f32[8,4096]{1,0:T(8,128)}, u32[]{:S(2)}) copy-start(f32[8,4096]{1,0:T(8,128)} %param.8) | copy-start | bytes 393220
  10.2 8.0 %copy-start.4 = (s32[4,128]{1,0:T(4,128)S(1)}, s32[4,128]{1,0:T(4,128)}, u32[]{:S(2)}) copy-start(s32[4,128]{1,0:T(4,128)} %param.9) | copy-start | bytes 6148
  10.2 8.7 %copy-start.2 = (f32[4,128]{1,0:T(4,128)S(1)}, f32[4,128]{1,0:T(4,128)}, u32[]{:S(2)}) copy-start(f32[4,128]{1,0:T(4,128)} %param.11) | copy-start | bytes 6148
  10.3 8.7 %collective-permute-start.1 = (f32[6,1,4096]{2,0,1:T(8,128)S(1)}, f32[6,1,4096]{2,0,1:T(8,128)S(1)}, u32[]{:S(2)}, u32[]{:S(2)}) collective-permute-start(f32[6,1,4096]{2,0,1:T(8,128)S(1)} %get-tuple-element.41), channel_id=1, source_target_pairs={{0,1},{1,2},{2,3},{3,4},{4,5},{5,6},{6,7},{8,9},{9,10},{10,11},{11... | collective-permute-start | bytes 294920 | tf_op jit(solution)/shard_map/ppermute | solution.py:37
  15.2 6.9 %collective-permute-start = (f32[6,1,4096]{2,0,1:T(8,128)S(1)}, f32[6,1,4096]{2,0,1:T(8,128)S(1)}, u32[]{:S(2)}, u32[]{:S(2)}) collective-permute-start(f32[6,1,4096]{2,0,1:T(8,128)S(1)} %get-tuple-element.40), channel_id=1, source_target_pairs={{1,0},{2,1},{3,2},{4,3},{5,4},{6,5},{7,6},{9,8},{10,9},{11,10},{12... | collective-permute-start | bytes 294920 | tf_op jit(solution)/shard_map/ppermute | solution.py:39
  25.1 7.2 %collective-permute-start.3 = (f32[6,1,4096]{2,0,1:T(8,128)S(1)}, f32[6,1,4096]{2,0,1:T(8,128)S(1)}, u32[]{:S(2)}, u32[]{:S(2)}) collective-permute-start(f32[6,1,4096]{2,0,1:T(8,128)S(1)} %get-tuple-element.31), channel_id=1, source_target_pairs={{0,1},{1,2},{2,3},{3,4},{4,5},{5,6},{6,7},{8,9},{9,10},{10,11},{11... | collective-permute-start | bytes 294920 | tf_op jit(solution)/shard_map/ppermute | solution.py:37
  29.5 6.9 %collective-permute-start.2 = (f32[6,1,4096]{2,0,1:T(8,128)S(1)}, f32[6,1,4096]{2,0,1:T(8,128)S(1)}, u32[]{:S(2)}, u32[]{:S(2)}) collective-permute-start(f32[6,1,4096]{2,0,1:T(8,128)S(1)} %get-tuple-element.30), channel_id=1, source_target_pairs={{1,0},{2,1},{3,2},{4,3},{5,4},{6,5},{7,6},{9,8},{10,9},{11,10},{12... | collective-permute-start | bytes 294920 | tf_op jit(solution)/shard_map/ppermute | solution.py:39
  37.1 7.9 %collective-permute-start.5 = (f32[6,1,4096]{2,0,1:T(8,128)S(1)}, f32[6,1,4096]{2,0,1:T(8,128)S(1)}, u32[]{:S(2)}, u32[]{:S(2)}) collective-permute-start(f32[6,1,4096]{2,0,1:T(8,128)S(1)} %get-tuple-element.29), channel_id=1, source_target_pairs={{0,1},{1,2},{2,3},{3,4},{4,5},{5,6},{6,7},{8,9},{9,10},{10,11},{11... | collective-permute-start | bytes 294920 | tf_op jit(solution)/shard_map/ppermute | solution.py:37
  41.1 6.9 %collective-permute-start.4 = (f32[6,1,4096]{2,0,1:T(8,128)S(1)}, f32[6,1,4096]{2,0,1:T(8,128)S(1)}, u32[]{:S(2)}, u32[]{:S(2)}) collective-permute-start(f32[6,1,4096]{2,0,1:T(8,128)S(1)} %get-tuple-element.28), channel_id=1, source_target_pairs={{1,0},{2,1},{3,2},{4,3},{5,4},{6,5},{7,6},{9,8},{10,9},{11,10},{12... | collective-permute-start | bytes 294920 | tf_op jit(solution)/shard_map/ppermute | solution.py:39
  50.8 21.6 %copy-start.1 = (f32[6,4,128]{2,1,0:T(4,128)S(1)}, f32[6,4,128]{2,1,0:T(4,128)}, u32[]{:S(2)}) copy-start(f32[6,4,128]{2,1,0:T(4,128)} %param.12) | copy-start | bytes 36868
  50.8 21.6 %copy-start.3 = (f32[4,128]{1,0:T(4,128)S(1)}, f32[4,128]{1,0:T(4,128)}, u32[]{:S(2)}) copy-start(f32[4,128]{1,0:T(4,128)} %param.10) | copy-start | bytes 6148
  73.0 13.7 %all-to-all-start = ((f32[4,6,512]{2,1,0:T(8,128)}), f32[4,6,512]{2,1,0:T(8,128)S(1)}, u32[]{:S(2)}, u32[]{:S(2)}) async-start(f32[4,6,512]{2,1,0:T(8,128)} %stack.19), calls=%async_computation | async-start | bytes 131072 | tf_op jit(solution)/shard_map/all_to_all | solution.py:16
  76.3 150.3 %reduce-scatter.2.cloned.1.call-start = ((), (), s32[]{:S(2)}) async-start(), calls=%async_computation.2 | async-start | bytes 11796480 | tf_op jit(solution)/shard_map/reduce_scatter | solution.py:131
  76.5 54.7 %collective-permute-start.7 = (f32[6,1,4096]{2,0,1:T(8,128)}, f32[6,1,4096]{2,0,1:T(8,128)S(1)}, u32[]{:S(2)}, u32[]{:S(2)}) collective-permute-start(f32[6,1,4096]{2,0,1:T(8,128)} %get-tuple-element.23), channel_id=1, source_target_pairs={{0,1},{1,2},{2,3},{3,4},{4,5},{5,6},{6,7},{8,9},{9,10},{10,11},{11... | collective-permute-start | bytes 294920 | tf_op jit(solution)/shard_map/ppermute | solution.py:37
  80.2 50.9 %collective-permute-start.6 = (f32[6,1,4096]{2,0,1:T(8,128)}, f32[6,1,4096]{2,0,1:T(8,128)}, u32[]{:S(2)}, u32[]{:S(2)}) collective-permute-start(f32[6,1,4096]{2,0,1:T(8,128)} %get-tuple-element.22), channel_id=1, source_target_pairs={{1,0},{2,1},{3,2},{4,3},{5,4},{6,5},{7,6},{9,8},{10,9},{11,10},{12... | collective-permute-start | bytes 294920 | tf_op jit(solution)/shard_map/ppermute | solution.py:39
Sparse Core Ops, SparseCore 0:
  151.0 75.6 reduce-scatter.1
